TPU v7x, 32 devices: a whole 2x2x4 slice. The times are simulated.
32 devices in a mesh: band: 8 (over z, x), cuts: 4 (over y, core).
Axes of the slice: x: 2, y: 2, z: 4, core: 2. Of those that a mesh axis runs over, the one named last changes fastest.
Arguments:
- var_feat: bfloat16 [163840, 128], P(('band', 'cuts')), may hold values from -6 to 6
- con_feat: bfloat16 [4096, 128], P(('band', 'cuts')), may hold values from -6 to 6
- slot_column_block: int32 [5120], P(('band', 'cuts')), may hold values from 0 to 39
- slot_constraint_block: int32 [5120], P(('band', 'cuts')), may hold values from 0 to 7
- block_count: int32 [32], P(('band', 'cuts')), may hold values from 40 to 160, as said below
- incidence_coefficients: int32 [5120, 128, 128], P(('band', 'cuts')), may hold values from -3 to 4
- con_first: bfloat16 [256, 256], replicated, may hold values from -0.375 to 0.375
- con_bias: float32 [256], replicated, may hold values from -3 to 3
- con_second: bfloat16 [256, 256], replicated, may hold values from -0.375 to 0.375
- con_third: bfloat16 [256, 128], replicated, may hold values from -0.375 to 0.375
- con_gain: float32 [128], replicated, may hold values from 0.1 to 1.9
- con_shift: float32 [128], replicated, may hold values from -3 to 3
- var_first: bfloat16 [256, 256], replicated, may hold values from -0.375 to 0.375
- var_bias: float32 [256], replicated, may hold values from -3 to 3
- var_second: bfloat16 [256, 256], replicated, may hold values from -0.375 to 0.375
- var_third: bfloat16 [256, 128], replicated, may hold values from -0.375 to 0.375
- var_gain: float32 [128], replicated, may hold values from 0.1 to 1.9
- var_shift: float32 [128], replicated, may hold values from -3 to 3
Outputs:
- con_new: bfloat16 [4096, 128], P(('band', 'cuts'))
- var_new: bfloat16 [163840, 128], P(('band', 'cuts'))
Inputs may be any that keep to these rules, and one draw needn't show every extreme that they name: Each device's live slots are its first block_count slots; in every draw one eighth of the devices hold 160 live slots and some device holds 40.
All inputs are finite; a program needn't handle non-finite values.
Results may differ from a plain program's by a relative error of at most 0.0075.
Values may be sent and summed in bfloat16 or wider, within the bound.
A program may use at most 128 MiB of HBM per device.

v0:
```python
import math

import jax
import jax.numpy as jnp
from jax import lax
from jax.sharding import PartitionSpec as P

EPS = 1e-05


def passed_along(array, axis, by):
    size = lax.axis_size(axis)
    pairs = [(i, i + by) for i in range(size) if 0 <= i + by < size]
    return lax.ppermute(array, axis, pairs)


def layer_norm(values, gain, offset):
    center = values - jnp.mean(values, axis=-1, keepdims=True)
    spread = jnp.mean(center * center, axis=-1, keepdims=True)
    return center * lax.rsqrt(spread + EPS) * gain + offset


def node_update(feats, scaled_agg, w_first, bias, w_second, w_third, gain, offset):
    joined = jnp.concatenate([feats, scaled_agg.astype(jnp.bfloat16)], axis=1)
    hidden = jnp.maximum(
        jnp.dot(joined, w_first, preferred_element_type=jnp.float32) + bias, 0.0
    ).astype(jnp.bfloat16)
    middle = jnp.maximum(jnp.dot(hidden, w_second, preferred_element_type=jnp.float32), 0.0).astype(
        jnp.bfloat16
    )
    output = jnp.dot(middle, w_third, preferred_element_type=jnp.float32)
    return layer_norm(feats.astype(jnp.float32) + output, gain, offset).astype(jnp.bfloat16)


def on_device(
    var_feat,
    con_feat,
    slot_column_block,
    slot_constraint_block,
    block_count,
    incidence_coefficients,
    con_first,
    con_bias,
    con_second,
    con_third,
    con_gain,
    con_shift,
    var_first,
    var_bias,
    var_second,
    var_third,
    var_gain,
    var_shift,
):
    width = var_feat.shape[1]
    slot_total = slot_column_block.shape[0]
    block_size = incidence_coefficients.shape[1]
    col_blocks = var_feat.shape[0] // block_size
    band_blocks = lax.axis_size("cuts") * (con_feat.shape[0] // block_size)
    highest = lax.Precision.HIGHEST
    coef_half = incidence_coefficients.astype(jnp.bfloat16)
    live = (jnp.arange(slot_total, dtype=jnp.int32) < block_count[0]).astype(jnp.float32)
    picked = jnp.take(var_feat.reshape(col_blocks, block_size, width), slot_column_block, axis=0)
    products = jnp.einsum("sij,sjw->siw", coef_half, picked, preferred_element_type=jnp.float32)
    row_ids = jnp.arange(2 * band_blocks, dtype=jnp.int32)
    selector = (slot_constraint_block[None, :] == row_ids[:, None]).astype(jnp.float32) * live[
        None, :
    ]
    partials = jnp.einsum("rs,siw->riw", selector, products, precision=highest)
    partials = partials.reshape(2, band_blocks * block_size, width)
    own_part = partials[0]
    link_part = partials[1]
    arriving = passed_along(link_part, "band", 1)
    con_agg = lax.psum_scatter(own_part + arriving, "cuts", scatter_dimension=0, tiled=True)
    con_agg = con_agg * (1.0 / math.sqrt(block_size * slot_total))
    con_new = node_update(
        con_feat, con_agg, con_first, con_bias, con_second, con_third, con_gain, con_shift
    )
    band_feat = lax.all_gather(con_new, "cuts", axis=0, tiled=True)
    next_feat = passed_along(band_feat, "band", -1)
    window = jnp.concatenate([band_feat, next_feat], axis=0).reshape(
        2 * band_blocks, block_size, width
    )
    picked_rows = jnp.take(window, slot_constraint_block, axis=0)
    back = jnp.einsum("sij,siw->sjw", coef_half, picked_rows, preferred_element_type=jnp.float32)
    col_ids = jnp.arange(col_blocks, dtype=jnp.int32)
    column_sel = (slot_column_block[None, :] == col_ids[:, None]).astype(jnp.float32) * live[
        None, :
    ]
    var_agg = jnp.einsum("cs,sjw->cjw", column_sel, back, precision=highest).reshape(
        col_blocks * block_size, width
    )
    var_agg = var_agg * (1.0 / math.sqrt(4 * block_size))
    var_new = node_update(
        var_feat, var_agg, var_first, var_bias, var_second, var_third, var_gain, var_shift
    )
    return (con_new, var_new)


def solution(mesh):
    in_specs = (
        P(("band", "cuts"), None),
        P(("band", "cuts"), None),
        P(("band", "cuts")),
        P(("band", "cuts")),
        P(("band", "cuts")),
        P(("band", "cuts"), None, None),
        P(),
        P(),
        P(),
        P(),
        P(),
        P(),
        P(),
        P(),
        P(),
        P(),
        P(),
        P(),
    )
    out_specs = (P(("band", "cuts"), None), P(("band", "cuts"), None))
    return jax.shard_map(
        on_device, mesh=mesh, in_specs=in_specs, out_specs=out_specs, check_vma=False
    )
```

profile of v0, /device:TPU:0, one launch (start us, length us, event | category | flops | bytes accessed | tf_op | source)
XLA Modules:
  0.0 156.6 jit_solution(12916443900566128418)
XLA Ops:
  7.2 0.0 copy-start
  7.2 0.0 reduce-scatter.2.cloned.1.call-start
  7.2 0.7 compare_select_fusion.1
  7.9 0.7 compare_and_fusion.1
  9.3 9.1 %gather_fusion = bf16[160,128,128]{2,1,0:T(8,128)(2,1)} fusion(bf16[40,128,128]{2,1,0:T(8,128)(2,1)} %bitcast.31, s32[1024]{0:T(1024)S(1)} %pad_clamp_fusion.1), kind=kCustom, calls=%fused_computation | custom fusion | bytes 10486400 | tf_op jit(solution)/shard_map/jit(_take)/gather | solution.py:63
  18.4 13.4 %fusion.9 = f32[160,128,128]{2,1,0:T(8,128)} fusion(bf16[160,128,128]{2,1,0:T(8,128)(2,1)} %gather_fusion, pred[160]{0:T(512)(128)(4,1)S(1)} %compare_and_fusion.1, s32[160,128,128]{2,1,0:T(8,128)} %param.23), kind=kOutput, calls=%fused_computation.14 | convolution fusion | flops 676331520 | bytes 26214560 | tf_op jit(solution)/shard_map/sij,sjw->siw/dot_general | solution.py:64
  31.8 0.0 copy-start.4
  31.8 11.5 %copy.32 = f32[160,128,128]{1,0,2:T(8,128)} copy(f32[160,128,128]{2,1,0:T(8,128)} %fusion.9) | data formatting | bytes 20971520 | tf_op jit(solution)/shard_map/sij,sjw->siw/dot_general | solution.py:64
  43.3 0.0 copy-done.4
  43.3 0.0 copy-start.3
  43.3 0.0 copy-start.10
  43.3 0.0 copy-start.11
  43.3 0.0 copy-start.14
  43.3 0.0 copy-start.2
  43.3 0.0 copy-start.6
  43.3 0.0 copy-start.7
  43.4 0.0 copy-start.1
  43.4 7.8 %fusion.2 = f32[8,128,128]{2,0,1:T(8,128)S(1)} fusion(f32[160,128,128]{1,0,2:T(8,128)} %copy.32, f32[160]{0:T(256)S(1)} %compare_convert_fusion, s32[160]{0:T(256)S(1)} %copy-done.4), kind=kOutput, calls=%fused_computation.4 | convolution fusion | flops 251660800 | bytes 11011328 | tf_op jit(solution)/shard_map/rs,siw->riw/dot_general | solution.py:69
  51.1 0.1 fusion.52
  51.3 4.9 %collective-permute-start = (f32[512,128]{1,0:T(8,128)S(1)}, f32[512,128]{1,0:T(8,128)S(1)}, u32[]{:S(2)}, u32[]{:S(2)}) collective-permute-start(f32[512,128]{1,0:T(8,128)S(1)} %bitcast.33), channel_id=1, source_target_pairs={{0,4},{4,8},{8,12},{12,16},{16,20},{20,24},{24,28},{1,5},{5,9},{9,... | collective-permute-start | bytes 786440 | tf_op jit(solution)/shard_map/ppermute | solution.py:14
  56.2 5.5 %collective-permute-done = f32[512,128]{1,0:T(8,128)S(1)} collective-permute-done((f32[512,128]{1,0:T(8,128)S(1)}, f32[512,128]{1,0:T(8,128)S(1)}, u32[]{:S(2)}, u32[]{:S(2)}) %collective-permute-start) | collective-permute-done | bytes 262176 | tf_op jit(solution)/shard_map/ppermute | solution.py:14
  61.7 0.7 bitcast_add_fusion
  62.4 0.0 reduce-scatter.2.cloned.1.call-update
  62.4 0.0 copy-done.3
  62.4 0.1 copy.24
  62.6 22.3 %reduce-scatter.2.cloned.1.call-done = f32[128,128]{1,0:T(8,128)} async-done(((f32[512,128]{1,0:T(8,128)}), f32[128,128]{1,0:T(8,128)}) %reduce-scatter.2.cloned.1.call-update) | async-done | bytes 65552 | tf_op jit(solution)/shard_map/reduce_scatter | solution.py:74
  84.9 0.8 multiply_convert_fusion.1
  85.7 0.0 copy-done.10
  85.7 0.0 copy-done.11
  85.8 0.0 copy-done.14
  85.8 0.3 fusion.24
  86.1 0.0 copy-done.2
  86.1 0.2 fusion.53
  86.4 0.0 copy-done.6
  86.4 0.0 copy-done.7
  86.4 0.1 add_convert_fusion.1
  86.5 5.4 %all_gather.3 = bf16[512,128]{0,1:T(8,128)(2,1)S(1)} all-gather(bf16[128,128]{0,1:T(8,128)(2,1)S(1)} %add_convert_fusion.1), channel_id=1, replica_groups=mesh['band'=8,'cuts'=4] {'cuts'}, dimensions={0}, use_global_device_ids=true | all-gather | bytes 163840 | tf_op jit(solution)/shard_map/all_gather | solution.py:79
  91.9 1.5 collective-permute-start.1
  93.4 0.0 copy-done.1
  93.4 1.4 copy.27
  94.9 0.7 copy.30
  95.6 4.0 %collective-permute-done.1 = bf16[512,128]{0,1:T(8,128)(2,1)S(1)} collective-permute-done((bf16[512,128]{0,1:T(8,128)(2,1)S(1)}, bf16[512,128]{0,1:T(8,128)(2,1)S(1)}, u32[]{:S(2)}, u32[]{:S(2)}) %collective-permute-start.1) | collective-permute-done | bytes 131104 | tf_op jit(solution)/shard_map/ppermute | solution.py:14
  99.6 0.2 copy.34
  99.8 7.7 %gather_fusion.1 = bf16[160,128,128]{2,1,0:T(8,128)(2,1)} fusion(bf16[8,128,128]{2,1,0:T(8,128)(2,1)S(1)} %bitcast.30, s32[1024]{0:T(1024)S(1)} %pad_clamp_fusion), kind=kCustom, calls=%fused_computation.1 | custom fusion | bytes 10486400 | tf_op jit(solution)/shard_map/jit(_take)/gather | solution.py:84
  107.5 11.6 %fusion.7 = f32[160,128,128]{2,1,0:T(8,128)} fusion(bf16[160,128,128]{2,1,0:T(8,128)(2,1)} %gather_fusion.1, pred[160]{0:T(512)(128)(4,1)S(1)} %compare_and_fusion, s32[160,128,128]{2,1,0:T(8,128)} %param.23), kind=kOutput, calls=%fused_computation.12 | convolution fusion | flops 676331520 | bytes 26214560 | tf_op jit(solution)/shard_map/sij,siw->sjw/dot_general | solution.py:85
  119.1 0.0 copy-start.5
  119.1 11.5 %copy.33 = f32[160,128,128]{1,0,2:T(8,128)} copy(f32[160,128,128]{2,1,0:T(8,128)} %fusion.7) | data formatting | bytes 20971520 | tf_op jit(solution)/shard_map/sij,siw->sjw/dot_general | solution.py:85
  130.6 0.0 copy-done.5
  130.6 0.0 copy-start.15
  130.6 8.2 %multiply_convert_fusion = bf16[40,128,128]{2,0,1:T(8,128)(2,1)S(1)} fusion(f32[160,128,128]{1,0,2:T(8,128)} %copy.33, f32[160]{0:T(256)S(1)} %compare_convert_fusion, s32[160]{0:T(256)S(1)} %copy-done.5), kind=kOutput, calls=%fused_computation.23 | convolution fusion | flops 1259614720 | bytes 11797760 | tf_op jit(solution)/shard_map/cs,sjw->cjw/dot_general | solution.py:90
  138.9 0.3 copy.29
  139.2 0.0 copy-done
  139.2 0.0 copy-done.15
  139.2 0.0 copy-start.12
  139.2 0.0 copy-start.13
  139.2 2.4 %fusion.6 = bf16[5120,256]{1,0:T(8,128)(2,1)} fusion(bf16[256,256]{1,0:T(8,128)(2,1)S(1)} %copy-done, bf16[5120,128]{1,0:T(8,128)(2,1)S(1)} %bitcast.32, bf16[5120,128]{1,0:T(8,128)(2,1)S(1)} %copy-done.1, f32[256]{0:T(256)S(1)} %copy-done.15), kind=kOutput, calls=%fused_computation.10 | convolution fusion | flops 680263680 | bytes 5374976 | tf_op jit(solution)/shard_map/dot_general | solution.py:26
  141.6 0.0 copy-done.12
  141.6 0.0 copy-done.13
  141.6 3.8 %fusion.54 = (f32[5120]{0:T(1024)S(1)}, f32[5120,128]{0,1:T(8,128)S(1)}) fusion(bf16[256,128]{1,0:T(8,128)(2,1)S(1)} %copy-done.13, bf16[5120,256]{1,0:T(8,128)(2,1)} %fusion.6, bf16[256,256]{1,0:T(8,128)(2,1)S(1)} %copy-done.12, bf16[5120,128]{0,1:T(8,128)(2,1)} %copy.27), kind=kOutput, calls=%fused_computation.77 | convolution fusion | flops 1011215360 | bytes 6770688 | tf_op jit(solution)/shard_map/dot_general | solution.py:31
  145.5 0.3 multiply_reduce_fusion
  145.8 0.0 copy-done.8
  145.8 0.0 copy-done.9
  145.8 1.6 add_convert_fusion
  147.4 2.4 %copy.31 = bf16[5120,128]{1,0:T(8,128)(2,1)} copy(bf16[5120,128]{0,1:T(8,128)(2,1)} %add_convert_fusion) | data formatting | bytes 2621440
  (15 shorter events, 0.2 us)
Async XLA Ops:
  7.2 132.0 %copy-start = (bf16[256,256]{1,0:T(8,128)(2,1)S(1)}, bf16[256,256]{1,0:T(8,128)(2,1)}, u32[]{:S(2)}) copy-start(bf16[256,256]{1,0:T(8,128)(2,1)} %param.30) | copy-start | bytes 393220
  7.2 77.7 %reduce-scatter.2.cloned.1.call-start = ((), (), s32[]{:S(2)}) async-start(), calls=%async_computation.1 | async-start | bytes 327680 | tf_op jit(solution)/shard_map/reduce_scatter | solution.py:74
  31.8 11.5 %copy-start.4 = (s32[160]{0:T(256)S(1)}, s32[160]{0:T(256)}, u32[]{:S(2)}) copy-start(s32[160]{0:T(256)} %param.21) | copy-start | bytes 1924
  43.3 19.1 %copy-start.3 = (bf16[128,128]{1,0:T(8,128)(2,1)S(1)}, bf16[128,128]{1,0:T(8,128)(2,1)}, u32[]{:S(2)}) copy-start(bf16[128,128]{1,0:T(8,128)(2,1)} %param.19) | copy-start | bytes 98308
  43.3 42.4 %copy-start.10 = (bf16[256,256]{1,0:T(8,128)(2,1)S(1)}, bf16[256,256]{1,0:T(8,128)(2,1)}, u32[]{:S(2)}) copy-start(bf16[256,256]{1,0:T(8,128)(2,1)} %param.26) | copy-start | bytes 393220
  43.3 42.4 %copy-start.11 = (bf16[256,256]{1,0:T(8,128)(2,1)S(1)}, bf16[256,256]{1,0:T(8,128)(2,1)}, u32[]{:S(2)}) copy-start(bf16[256,256]{1,0:T(8,128)(2,1)} %param.24) | copy-start | bytes 393220
  43.3 42.4 %copy-start.14 = (f32[256]{0:T(256)S(1)}, f32[256]{0:T(256)}, u32[]{:S(2)}) copy-start(f32[256]{0:T(256)} %param.25) | copy-start | bytes 3076
  43.3 42.7 %copy-start.2 = (bf16[256,128]{1,0:T(8,128)(2,1)S(1)}, bf16[256,128]{1,0:T(8,128)(2,1)}, u32[]{:S(2)}) copy-start(bf16[256,128]{1,0:T(8,128)(2,1)} %param.27) | copy-start | bytes 196612
  43.3 43.0 %copy-start.6 = (f32[128]{0:T(128)S(1)}, f32[128]{0:T(128)}, u32[]{:S(2)}) copy-start(f32[128]{0:T(128)} %param.29) | copy-start | bytes 1540
  43.3 43.0 %copy-start.7 = (f32[128]{0:T(128)S(1)}, f32[128]{0:T(128)}, u32[]{:S(2)}) copy-start(f32[128]{0:T(128)} %param.28) | copy-start | bytes 1540
  43.4 50.1 %copy-start.1 = (bf16[5120,128]{1,0:T(8,128)(2,1)S(1)}, bf16[5120,128]{1,0:T(8,128)(2,1)}, u32[]{:S(2)}) copy-start(bf16[5120,128]{1,0:T(8,128)(2,1)} %param.18) | copy-start | bytes 3932164
  51.3 10.4 %collective-permute-start = (f32[512,128]{1,0:T(8,128)S(1)}, f32[512,128]{1,0:T(8,128)S(1)}, u32[]{:S(2)}, u32[]{:S(2)}) collective-permute-start(f32[512,128]{1,0:T(8,128)S(1)} %bitcast.33), channel_id=1, source_target_pairs={{0,4},{4,8},{8,12},{12,16},{16,20},{20,24},{24,28},{1,5},{5,9},{9,... | collective-permute-start | bytes 786440 | tf_op jit(solution)/shard_map/ppermute | solution.py:14
  91.9 7.6 %collective-permute-start.1 = (bf16[512,128]{0,1:T(8,128)(2,1)S(1)}, bf16[512,128]{0,1:T(8,128)(2,1)S(1)}, u32[]{:S(2)}, u32[]{:S(2)}) collective-permute-start(bf16[512,128]{0,1:T(8,128)(2,1)S(1)} %all_gather.3), channel_id=1, source_target_pairs={{4,0},{8,4},{12,8},{16,12},{20,16},{24,20},{28,24},{5,1},{9,5},{13... | collective-permute-start | bytes 393224 | tf_op jit(solution)/shard_map/ppermute | solution.py:14
  119.1 11.5 %copy-start.5 = (s32[160]{0:T(256)S(1)}, s32[160]{0:T(256)}, u32[]{:S(2)}) copy-start(s32[160]{0:T(256)} %param.20) | copy-start | bytes 1924
  130.6 8.6 %copy-start.15 = (f32[256]{0:T(256)S(1)}, f32[256]{0:T(256)}, u32[]{:S(2)}) copy-start(f32[256]{0:T(256)} %param.31) | copy-start | bytes 3076
  139.2 2.4 %copy-start.12 = (bf16[256,256]{1,0:T(8,128)(2,1)S(1)}, bf16[256,256]{1,0:T(8,128)(2,1)}, u32[]{:S(2)}) copy-start(bf16[256,256]{1,0:T(8,128)(2,1)} %param.32) | copy-start | bytes 393220
  139.2 2.4 %copy-start.13 = (bf16[256,128]{1,0:T(8,128)(2,1)S(1)}, bf16[256,128]{1,0:T(8,128)(2,1)}, u32[]{:S(2)}) copy-start(bf16[256,128]{1,0:T(8,128)(2,1)} %param.33) | copy-start | bytes 196612
  141.6 4.2 %copy-start.8 = (f32[128]{0:T(128)S(1)}, f32[128]{0:T(128)}, u32[]{:S(2)}) copy-start(f32[128]{0:T(128)} %param.35) | copy-start | bytes 1540
  141.6 4.2 %copy-start.9 = (f32[128]{0:T(128)S(1)}, f32[128]{0:T(128)}, u32[]{:S(2)}) copy-start(f32[128]{0:T(128)} %param.34) | copy-start | bytes 1540
Sparse Core Ops, SparseCore 0:
  62.6 22.2 reduce-scatter.1
where the time goes:
time: 157 us
  matrix products  47.8 us (30%)
  local copies, waits for them, and re-layouts  45.2 us (29%)
  waiting for transfers between devices  31.8 us (20%)
  between operations  15 us (10%)
  starting transfers between devices  6.37 us (4%)
  blocking collectives  5.45 us (3%)
  other arithmetic  5.05 us (3%)
    reduce_scatter x1, waiting for transfers between devices, on_device(): lax.psum_scatter(own_part + arriving, 'cuts', scatter_dimension=0, tiled=...  22.3 us
    dot_general x1, matrix products, on_device(): jnp.einsum('sij,sjw->siw', coef_half, picked, preferred_element_type=jnp....  13.4 us
    dot_general x1, matrix products, on_device(): jnp.einsum('sij,siw->sjw', coef_half, picked_rows, preferred_element_type...  11.6 us
    dot_general x1, local copies, waits for them, and re-layouts, on_device(): jnp.einsum('sij,sjw->siw', coef_half, picked, preferred_element_type=jnp....  11.5 us
    dot_general x1, local copies, waits for them, and re-layouts, on_device(): jnp.einsum('sij,siw->sjw', coef_half, picked_rows, preferred_element_type...  11.5 us
    ppermute x2, waiting for transfers between devices, passed_along(): return lax.ppermute(array, axis, pairs)  9.47 us
    gather x1, local copies, waits for them, and re-layouts, on_device(): jnp.take(var_feat.reshape(col_blocks, block_size, width), slot_column_blo...  9.06 us
    dot_general x1, matrix products, on_device(): jnp.einsum('cs,sjw->cjw', column_sel, back, precision=highest)  8.25 us
  transfers between devices with their start and end apart: 3, of which 3 were waited for; matrix products, arithmetic and copies ran while one was open for 1% of the time, Pallas kernels for 0%

commit v1 on v0

v1 whole, which is shorter than its diff:
```python
import functools
import math

import jax
import jax.numpy as jnp
from jax import lax
from jax.experimental import pallas as pl
from jax.experimental.pallas import tpu as pltpu
from jax.sharding import PartitionSpec as P

EPS = 1e-05
F32 = jnp.float32
BF16 = jnp.bfloat16
MESH = pl.DeviceIdType.MESH
CHUNK = 16
UNROLL = 8


def layer_norm(values, gain, offset):
    center = values - jnp.mean(values, axis=-1, keepdims=True)
    spread = jnp.mean(center * center, axis=-1, keepdims=True)
    return center * lax.rsqrt(spread + EPS) * gain + offset


def node_update(feats, scaled_agg, w_first, bias, w_second, w_third, gain, offset):
    joined = jnp.concatenate([feats, scaled_agg.astype(BF16)], axis=1)
    hidden = jnp.maximum(jnp.dot(joined, w_first, preferred_element_type=F32) + bias, 0.0).astype(BF16)
    middle = jnp.maximum(jnp.dot(hidden, w_second, preferred_element_type=F32), 0.0).astype(BF16)
    output = jnp.dot(middle, w_third, preferred_element_type=F32)
    return layer_norm(feats.astype(F32) + output, gain, offset).astype(BF16)


def order_rows(key_row, key_col, other_col, live_row, live_col, lanes, group):
    slots = key_col.shape[0]
    iota = lambda shape, axis: lax.broadcasted_iota(jnp.int32, shape, axis)
    lane = iota((slots, lanes), 1)
    before = (key_row == key_col) & (iota((slots, slots), 1) < iota((slots, slots), 0))
    within = jnp.sum(jnp.where(before, live_row, 0), axis=1, keepdims=True)
    counts = jnp.sum(jnp.where(lane == key_col, live_col, 0), axis=0, keepdims=True)
    counts_col = jnp.sum(jnp.where(iota((lanes, slots), 0) == key_row, live_row, 0), axis=1, keepdims=True)
    steps, steps_col = counts, counts_col
    if group == 2:
        steps, steps_col = (counts + 1) >> 1, (counts_col + 1) >> 1
    base_col = jnp.sum(jnp.where(lane < key_col, steps, 0), axis=1, keepdims=True)
    place = jnp.where(live_col > 0, base_col * group + within, -1)
    hit = place == lane
    index = jnp.sum(jnp.where(hit, iota((slots, lanes), 0) - slots, 0), axis=0, keepdims=True) + slots
    other = jnp.sum(jnp.where(hit, other_col, 0), axis=0, keepdims=True)
    opens = (place == lane * group) & (within == 0)
    carry = 1 - jnp.sum(jnp.where(opens, 1, 0), axis=0, keepdims=True)
    upto = iota((lanes, lanes), 0) <= iota((lanes, lanes), 1)
    ends = jnp.sum(jnp.where(upto, steps_col, 0), axis=0, keepdims=True)
    last = jnp.maximum(ends - 1, 0)
    filled = jnp.where(counts > 0, 1, 0)
    return [index, other, carry, last, filled]


def kernel(
    dims,
    cb_s, rb_s, cb_v, rb_v, count_s,
    vf_hbm, cf, coef_hbm,
    cw1, cbias, cw2, cw3, cgain, cshift,
    vw1, vbias, vw2, vw3, vgain, vshift,
    con_out, var_out,
    raw, half, prod, scan, paired, feat, result, part, arrive, window, conbuf,
    order_v, order_s,
    raw_sem, feat_sem, order_sem, out_sem, psend, precv, wsend, wrecv,
):
    nb, nc, slots, size, cols, pairs, lanes, chunks = dims
    band = lax.axis_index("band")
    cut = lax.axis_index("cuts")
    has_next = band < nb - 1
    has_prev = band > 0

    feat_copy = pltpu.make_async_copy(vf_hbm, feat, feat_sem)
    feat_copy.start()

    def raw_copy(i):
        piece = pl.ds(i * CHUNK, CHUNK)
        return pltpu.make_async_copy(coef_hbm.at[piece], raw.at[piece], raw_sem.at[i])

    for i in range(chunks):
        raw_copy(i).start()

    barrier = pltpu.get_barrier_semaphore()
    for d in range(1, nc):
        pl.semaphore_signal(barrier, inc=1, device_id=(band, lax.rem(cut + d, nc)), device_id_type=MESH)

    @pl.when(has_next)
    def _():
        for d in range(nc):
            pl.semaphore_signal(barrier, inc=1, device_id=(band + 1, lax.rem(cut + d, nc)), device_id_type=MESH)

    @pl.when(has_prev)
    def _():
        for d in range(nc):
            pl.semaphore_signal(barrier, inc=1, device_id=(band - 1, lax.rem(cut + d, nc)), device_id_type=MESH)

    row_c = cb_v[...]
    row_r = rb_v[...]
    diagonal = lax.broadcasted_iota(jnp.int32, (slots, slots), 0) == lax.broadcasted_iota(jnp.int32, (slots, slots), 1)
    col_c = jnp.sum(jnp.where(diagonal, row_c, 0), axis=1, keepdims=True)
    col_r = jnp.sum(jnp.where(diagonal, row_r, 0), axis=1, keepdims=True)
    count = count_s[0]
    live_row = jnp.where(lax.broadcasted_iota(jnp.int32, (1, slots), 1) < count, 1, 0)
    live_col = jnp.where(lax.broadcasted_iota(jnp.int32, (slots, 1), 0) < count, 1, 0)
    rows = order_rows(row_r, col_r, col_c, live_row, live_col, lanes, 1)
    rows += order_rows(row_c, col_c, col_r, live_row, live_col, lanes, 2)
    rows += [jnp.zeros((1, lanes), jnp.int32)] * (16 - len(rows))
    order_v[...] = jnp.concatenate(rows, axis=0)
    order_copy = pltpu.make_async_copy(order_v, order_s, order_sem)
    order_copy.start()

    half[slots] = jnp.zeros((size, size), BF16)
    prod[slots] = jnp.zeros((size, prod.shape[2]), F32)

    @pl.when(jnp.logical_not(has_prev))
    def _():
        arrive[pl.ds(nc, nc)] = jnp.zeros((nc,) + arrive.shape[1:], BF16)

    @pl.when(jnp.logical_not(has_next))
    def _():
        window[pl.ds(nc, nc)] = jnp.zeros((nc,) + window.shape[1:], BF16)

    feat_copy.wait()

    def forward(i, _):
        raw_copy(i).wait()

        def some(j, _):
            for u in range(UNROLL):
                s = i * CHUNK + j * UNROLL + u
                a = raw[s].astype(F32).astype(BF16)
                half[s] = a
                prod[s] = jnp.dot(a, feat[cb_s[s]], preferred_element_type=F32)
            return 0

        lax.fori_loop(0, CHUNK // UNROLL, some, 0)
        return 0

    lax.fori_loop(0, chunks, forward, 0)
    order_copy.wait()

    def sum_slots(k, carry):
        for u in range(4):
            at = k * 4 + u
            carry = carry * order_s[2, at].astype(F32) + prod[order_s[0, at]]
            scan[at] = carry
        return carry

    lax.fori_loop(0, slots // 4, sum_slots, jnp.zeros(prod.shape[1:], F32))

    blocks = part.shape[1] // size

    def fill(q):
        for e in range(blocks):
            r = q * blocks + e
            part[q, e * size : (e + 1) * size] = (scan[order_s[3, r]] * order_s[4, r].astype(F32)).astype(BF16)

    def part_send(d, ahead):
        to = lax.rem(cut + d, nc)
        q = ahead * nc + d
        return pltpu.make_async_remote_copy(
            src_ref=part.at[ahead * nc + to], dst_ref=arrive.at[ahead * nc + cut],
            send_sem=psend.at[q], recv_sem=precv.at[ahead * nc + cut],
            device_id=(band + ahead, to), device_id_type=MESH)

    def part_wait(src, ahead):
        pltpu.make_async_remote_copy(
            src_ref=part.at[0], dst_ref=arrive.at[ahead * nc + src],
            send_sem=psend.at[0], recv_sem=precv.at[ahead * nc + src],
            device_id=(band, cut), device_id_type=MESH).wait_recv()

    for q in range(2 * nc):
        fill(q)

    expected = (nc - 1) + jnp.where(has_next, nc, 0) + jnp.where(has_prev, nc, 0)
    pl.semaphore_wait(barrier, expected)

    @pl.when(has_next)
    def _():
        for d in range(nc):
            part_send(d, 1).start()

    for d in range(1, nc):
        part_send(d, 0).start()

    def pair_up(p, _):
        for u in range(2):
            k = p * 2 + u
            left = half[order_s[5, 2 * k]].T
            right = half[order_s[5, 2 * k + 1]].T
            paired[k, :, :size] = left
            paired[k, :, size:] = right
        return 0

    lax.fori_loop(0, pairs // 4, pair_up, 0)

    total = part[cut].astype(F32)
    for d in range(1, nc):
        src = lax.rem(cut + d, nc)
        part_wait(src, 0)
        total += arrive[src].astype(F32)

    @pl.when(has_prev)
    def _():
        for src in range(nc):
            part_wait(src, 1)

    for src in range(nc):
        total += arrive[nc + src].astype(F32)

    con_new = node_update(
        cf[...], total * (1.0 / math.sqrt(size * slots)), cw1[...], cbias[...], cw2[...], cw3[...], cgain[...], cshift[...])
    conbuf[...] = con_new
    con_out[...] = con_new
    window[cut] = con_new

    def win_send(d, back):
        to = lax.rem(cut + d, nc)
        return pltpu.make_async_remote_copy(
            src_ref=conbuf, dst_ref=window.at[back * nc + cut],
            send_sem=wsend.at[back * nc + d], recv_sem=wrecv.at[back * nc + cut],
            device_id=(band - back, to), device_id_type=MESH)

    def win_wait(src, back):
        pltpu.make_async_remote_copy(
            src_ref=conbuf, dst_ref=window.at[back * nc + src],
            send_sem=wsend.at[0], recv_sem=wrecv.at[back * nc + src],
            device_id=(band, cut), device_id_type=MESH).wait_recv()

    @pl.when(has_prev)
    def _():
        for d in range(nc):
            win_send(d, 1).start()

    for d in range(1, nc):
        win_send(d, 0).start()

    lax.fori_loop(pairs // 4, pairs // 2, pair_up, 0)

    @pl.when(has_next)
    def _():
        for d in range(nc):
            part_send(d, 1).wait_send()

    for d in range(1, nc):
        part_send(d, 0).wait_send()
        win_wait(lax.rem(cut + d, nc), 0)

    @pl.when(has_next)
    def _():
        for src in range(nc):
            win_wait(src, 1)

    def row_block(r):
        if blocks == 1:
            return window[r]
        return window[r // blocks, pl.ds(pl.multiple_of(r % blocks * size, size), size)]

    def back(k, carry):
        for u in range(4):
            at = k * 4 + u
            right = jnp.concatenate([row_block(order_s[6, 2 * at]), row_block(order_s[6, 2 * at + 1])], axis=0)
            term = jnp.dot(paired[at], right, preferred_element_type=F32)
            carry = carry * order_s[7, at].astype(F32) + term
            scan[at] = carry
        return carry

    lax.fori_loop(0, pairs // 4, back, jnp.zeros(scan.shape[1:], F32))

    scale = 1.0 / math.sqrt(4 * size)
    w1, w2, w3 = vw1[...], vw2[...], vw3[...]
    bias, gain, shift = vbias[...], vgain[...], vshift[...]

    def out_copy(i):
        piece = pl.ds(i * 2, 2)
        return pltpu.make_async_copy(result.at[piece], var_out.at[piece], out_sem.at[i])

    def update(i, _):
        feats, aggs = [], []
        for u in range(2):
            c = i * 2 + u
            feats.append(feat[c])
            aggs.append(scan[order_s[8, c]] * (order_s[9, c].astype(F32) * scale))
        new = node_update(
            jnp.concatenate(feats, axis=0), jnp.concatenate(aggs, axis=0), w1, bias, w2, w3, gain, shift)
        result[i * 2] = new[:size]
        result[i * 2 + 1] = new[size:]
        out_copy(i).start()
        return 0

    lax.fori_loop(0, cols // 2, update, 0)

    @pl.when(has_prev)
    def _():
        for d in range(nc):
            win_send(d, 1).wait_send()

    for d in range(1, nc):
        win_send(d, 0).wait_send()

    def finish(i, _):
        out_copy(i).wait()
        return 0

    lax.fori_loop(0, cols // 2, finish, 0)


def on_device(
    nb, nc,
    var_feat, con_feat, slot_column_block, slot_constraint_block, block_count, incidence_coefficients,
    con_first, con_bias, con_second, con_third, con_gain, con_shift,
    var_first, var_bias, var_second, var_third, var_gain, var_shift,
):
    width = var_feat.shape[1]
    slots = slot_column_block.shape[0]
    size = incidence_coefficients.shape[1]
    cols = var_feat.shape[0] // size
    rows = con_feat.shape[0]
    pairs = -(-(slots + cols) // 8) * 4
    lanes = -(-max(2 * pairs, slots) // 128) * 128
    chunks = slots // CHUNK
    dims = (nb, nc, slots, size, cols, pairs, lanes, chunks)
    smem = pl.BlockSpec(memory_space=pltpu.SMEM)
    vmem = pl.BlockSpec(memory_space=pltpu.VMEM)
    hbm = pl.BlockSpec(memory_space=pl.ANY)
    row = lambda v: v.reshape(1, -1)
    con_new, var_new = pl.pallas_call(
        functools.partial(kernel, dims),
        out_shape=(
            jax.ShapeDtypeStruct(con_feat.shape, BF16),
            jax.ShapeDtypeStruct((cols, size, width), BF16),
        ),
        in_specs=[smem, smem, vmem, vmem, smem, hbm, vmem, hbm] + [vmem] * 12,
        out_specs=(vmem, hbm),
        scratch_shapes=[
            pltpu.VMEM((slots, size, size), jnp.int32),
            pltpu.VMEM((slots + 1, size, size), BF16),
            pltpu.VMEM((slots + 1, size, width), F32),
            pltpu.VMEM((max(slots, pairs), size, width), F32),
            pltpu.VMEM((pairs, size, 2 * size), BF16),
            pltpu.VMEM((cols, size, width), BF16),
            pltpu.VMEM((cols, size, width), BF16),
            pltpu.VMEM((2 * nc, rows, width), BF16),
            pltpu.VMEM((2 * nc, rows, width), BF16),
            pltpu.VMEM((2 * nc, rows, width), BF16),
            pltpu.VMEM((rows, width), BF16),
            pltpu.VMEM((16, lanes), jnp.int32),
            pltpu.SMEM((16, lanes), jnp.int32),
            pltpu.SemaphoreType.DMA((chunks,)),
            pltpu.SemaphoreType.DMA,
            pltpu.SemaphoreType.DMA,
            pltpu.SemaphoreType.DMA((cols // 2,)),
            pltpu.SemaphoreType.DMA((2 * nc,)),
            pltpu.SemaphoreType.DMA((2 * nc,)),
            pltpu.SemaphoreType.DMA((2 * nc,)),
            pltpu.SemaphoreType.DMA((2 * nc,)),
        ],
        compiler_params=pltpu.CompilerParams(
            collective_id=0, has_side_effects=True, vmem_limit_bytes=63 * 1024 * 1024),
        name="layer",
    )(
        slot_column_block, slot_constraint_block, row(slot_column_block), row(slot_constraint_block), block_count,
        var_feat.reshape(cols, size, width), con_feat, incidence_coefficients,
        con_first, row(con_bias), con_second, con_third, row(con_gain), row(con_shift),
        var_first, row(var_bias), var_second, var_third, row(var_gain), row(var_shift),
    )
    return con_new, var_new.reshape(var_feat.shape)


def solution(mesh):
    both = P(("band", "cuts"))
    wide = P(("band", "cuts"), None)
    in_specs = (wide, wide, both, both, both, P(("band", "cuts"), None, None)) + (P(),) * 12
    body = functools.partial(on_device, mesh.shape["band"], mesh.shape["cuts"])
    return jax.shard_map(body, mesh=mesh, in_specs=in_specs, out_specs=(wide, wide), check_vma=False)
```

time: 157 us -> 48.6 us (0.31)
  matrix products: 47.8 us -> 0 us
  Pallas kernels: 0 us -> 43.2 us
  local copies, waits for them, and re-layouts: 45.2 us -> 3.83 us
  waiting for transfers between devices: 31.8 us -> 0 us
  between operations: 15 us -> 1.29 us
  starting transfers between devices: 6.37 us -> 0 us
  blocking collectives: 5.45 us -> 0 us
  other arithmetic: 5.05 us -> 0 us
    dot_general x8 -> x0, matrix products: 47.8 us -> none  [the longest x1 13.4 us: on_device(): jnp.einsum('sij,sjw->siw', coef_half, picked, preferred_element_type=jnp....]
    pallas_call x0 -> x1, Pallas kernels: none -> 43.2 us  [on_device(): pl.pallas_call(functools.partial(kernel, dims), out_shape=(jax.ShapeDtype...]
    dot_general x2 -> x0, local copies, waits for them, and re-layouts: 23 us -> none  [the longest x1 11.5 us: on_device(): jnp.einsum('sij,sjw->siw', coef_half, picked, preferred_element_type=jnp....]
    reduce_scatter x1 -> x0, waiting for transfers between devices: 22.3 us -> none  [on_device(): lax.psum_scatter(own_part + arriving, 'cuts', scatter_dimension=0, tiled=...]
    gather x2 -> x0, local copies, waits for them, and re-layouts: 16.8 us -> none  [the longest x1 9.06 us: on_device(): jnp.take(var_feat.reshape(col_blocks, block_size, width), slot_column_blo...]
    ppermute x2 -> x0, waiting for transfers between devices: 9.47 us -> none  [passed_along(): return lax.ppermute(array, axis, pairs)]
    ppermute x2 -> x0, starting transfers between devices: 6.33 us -> none  [passed_along(): return lax.ppermute(array, axis, pairs)]
    all_gather x1 -> x0, blocking collectives: 5.45 us -> none  [on_device(): band_feat = lax.all_gather(con_new, 'cuts', axis=0, tiled=True)]
  transfers between devices with their start and end apart: 3 -> 0, of which waited for: 3 -> 0; matrix products, arithmetic and copies ran while one was open for 1% -> 0% of each run, Pallas kernels for 0% -> 0%
where the time goes in v1:
time: 48.6 us; the launch traced here: 48.3 us
  Pallas kernels  43.2 us (89%)
  local copies, waits for them, and re-layouts  3.83 us (8%)
  between operations  1.29 us (3%)
    pallas_call x1, Pallas kernels, on_device(): pl.pallas_call(functools.partial(kernel, dims), out_shape=(jax.ShapeDtype...  43.2 us
    unnamed x2, local copies, waits for them, and re-layouts  3.83 us

profile of v1, /device:TPU:0, one launch (start us, length us, event | category | flops | bytes accessed | tf_op | source)
XLA Modules:
  0.0 48.3 jit_solution(3143852531209348360)
XLA Ops:
  1.3 43.2 %layer.1 = (bf16[128,128]{1,0:T(8,128)(2,1)}, bf16[40,128,128]{2,1,0:T(8,128)(2,1)}) custom-call(s32[160]{0:T(256)} %cb_s.1, s32[160]{0:T(256)} %rb_s.1, s32[1,160]{1,0:T(1,128)} %bitcast.12, s32[1,160]{1,0:T(1,128)} %bitcast.13, s32[1]{0:T(128)S(6)} %copy.22.count_s, bf16[40,128,128]{2,1,0:T(8,128)(2,1)} %bitcast.11, bf16[128,128]{1,0:T(8,128)(2,1)} %cf.1, ...), custom_call_target="tpu_custom_call" | custom-call | tf_op jit(solution)/shard_map/layer/pallas_call | solution.py:329
  44.5 1.4 %copy.23 = bf16[128,128]{1,0:T(8,128)(2,1)} copy(bf16[128,128]{1,0:T(8,128)(2,1)} %get-tuple-element.8) | data formatting | bytes 65536
  45.9 2.5 %copy.24 = bf16[5120,128]{1,0:T(8,128)(2,1)} copy(bf16[5120,128]{1,0:T(8,128)(2,1)} %bitcast.10) | data formatting | bytes 2621440

commit v2 on v1

--- a/solution.py
+++ b/solution.py
@@ -14,6 +14,9 @@
 MESH = pl.DeviceIdType.MESH
 CHUNK = 16
 UNROLL = 8
+FORWARD = 12
+BACK = 20
+STEP = 8
 
 
 def layer_norm(values, gain, offset):
@@ -62,11 +65,11 @@
     cw1, cbias, cw2, cw3, cgain, cshift,
     vw1, vbias, vw2, vw3, vgain, vshift,
     con_out, var_out,
-    raw, half, prod, scan, paired, feat, result, part, arrive, window, conbuf,
+    raw, half, scan, paired, feat, result, part, arrive, window, conbuf,
     order_v, order_s,
     raw_sem, feat_sem, order_sem, out_sem, psend, precv, wsend, wrecv,
 ):
-    nb, nc, slots, size, cols, pairs, lanes, chunks = dims
+    nb, nc, slots, size, cols, fpairs, pairs, lanes, chunks = dims
     band = lax.axis_index("band")
     cut = lax.axis_index("cuts")
     has_next = band < nb - 1
@@ -104,7 +107,7 @@
     count = count_s[0]
     live_row = jnp.where(lax.broadcasted_iota(jnp.int32, (1, slots), 1) < count, 1, 0)
     live_col = jnp.where(lax.broadcasted_iota(jnp.int32, (slots, 1), 0) < count, 1, 0)
-    rows = order_rows(row_r, col_r, col_c, live_row, live_col, lanes, 1)
+    rows = order_rows(row_r, col_r, col_c, live_row, live_col, lanes, 2)
     rows += order_rows(row_c, col_c, col_r, live_row, live_col, lanes, 2)
     rows += [jnp.zeros((1, lanes), jnp.int32)] * (16 - len(rows))
     order_v[...] = jnp.concatenate(rows, axis=0)
@@ -112,7 +115,6 @@
     order_copy.start()
 
     half[slots] = jnp.zeros((size, size), BF16)
-    prod[slots] = jnp.zeros((size, prod.shape[2]), F32)
 
     @pl.when(jnp.logical_not(has_prev))
     def _():
@@ -122,33 +124,33 @@
     def _():
         window[pl.ds(nc, nc)] = jnp.zeros((nc,) + window.shape[1:], BF16)
 
-    feat_copy.wait()
-
-    def forward(i, _):
+    def convert(i, _):
         raw_copy(i).wait()
 
         def some(j, _):
             for u in range(UNROLL):
-                s = i * CHUNK + j * UNROLL + u
-                a = raw[s].astype(F32).astype(BF16)
-                half[s] = a
-                prod[s] = jnp.dot(a, feat[cb_s[s]], preferred_element_type=F32)
+                at = i * CHUNK + j * UNROLL + u
+                half[at] = raw[at].astype(F32).astype(BF16)
             return 0
 
         lax.fori_loop(0, CHUNK // UNROLL, some, 0)
         return 0
 
-    lax.fori_loop(0, chunks, forward, 0)
+    lax.fori_loop(0, chunks, convert, 0)
+    feat_copy.wait()
     order_copy.wait()
 
-    def sum_slots(k, carry):
-        for u in range(4):
-            at = k * 4 + u
-            carry = carry * order_s[2, at].astype(F32) + prod[order_s[0, at]]
+    def forward(k, carry):
+        for u in range(FORWARD):
+            at = k * FORWARD + u
+            left = jnp.concatenate([half[order_s[0, 2 * at]], half[order_s[0, 2 * at + 1]]], axis=1)
+            right = jnp.concatenate([feat[order_s[1, 2 * at]], feat[order_s[1, 2 * at + 1]]], axis=0)
+            term = jnp.dot(left, right, preferred_element_type=F32)
+            carry = carry * order_s[2, at].astype(F32) + term
             scan[at] = carry
         return carry
 
-    lax.fori_loop(0, slots // 4, sum_slots, jnp.zeros(prod.shape[1:], F32))
+    lax.fori_loop(0, fpairs // FORWARD, forward, jnp.zeros(scan.shape[1:], F32))
 
     blocks = part.shape[1] // size
 
@@ -259,38 +261,35 @@
         return window[r // blocks, pl.ds(pl.multiple_of(r % blocks * size, size), size)]
 
     def back(k, carry):
-        for u in range(4):
-            at = k * 4 + u
+        for u in range(BACK):
+            at = k * BACK + u
             right = jnp.concatenate([row_block(order_s[6, 2 * at]), row_block(order_s[6, 2 * at + 1])], axis=0)
             term = jnp.dot(paired[at], right, preferred_element_type=F32)
             carry = carry * order_s[7, at].astype(F32) + term
             scan[at] = carry
         return carry
 
-    lax.fori_loop(0, pairs // 4, back, jnp.zeros(scan.shape[1:], F32))
+    lax.fori_loop(0, pairs // BACK, back, jnp.zeros(scan.shape[1:], F32))
 
     scale = 1.0 / math.sqrt(4 * size)
-    w1, w2, w3 = vw1[...], vw2[...], vw3[...]
-    bias, gain, shift = vbias[...], vgain[...], vshift[...]
-
     def out_copy(i):
-        piece = pl.ds(i * 2, 2)
+        piece = pl.ds(i * STEP, STEP)
         return pltpu.make_async_copy(result.at[piece], var_out.at[piece], out_sem.at[i])
 
     def update(i, _):
-        feats, aggs = [], []
-        for u in range(2):
-            c = i * 2 + u
-            feats.append(feat[c])
-            aggs.append(scan[order_s[8, c]] * (order_s[9, c].astype(F32) * scale))
-        new = node_update(
-            jnp.concatenate(feats, axis=0), jnp.concatenate(aggs, axis=0), w1, bias, w2, w3, gain, shift)
-        result[i * 2] = new[:size]
-        result[i * 2 + 1] = new[size:]
+        for u in range(0, STEP, 2):
+            c = i * STEP + u
+            feats = jnp.concatenate([feat[c], feat[c + 1]], axis=0)
+            aggs = [scan[order_s[8, c + e]] * (order_s[9, c + e].astype(F32) * scale) for e in range(2)]
+            new = node_update(
+                feats, jnp.concatenate(aggs, axis=0),
+                vw1[...], vbias[...], vw2[...], vw3[...], vgain[...], vshift[...])
+            result[c] = new[:size]
+            result[c + 1] = new[size:]
         out_copy(i).start()
         return 0
 
-    lax.fori_loop(0, cols // 2, update, 0)
+    lax.fori_loop(0, cols // STEP, update, 0)
 
     @pl.when(has_prev)
     def _():
@@ -304,7 +303,7 @@
         out_copy(i).wait()
         return 0
 
-    lax.fori_loop(0, cols // 2, finish, 0)
+    lax.fori_loop(0, cols // STEP, finish, 0)
 
 
 def on_device(
@@ -318,10 +317,12 @@
     size = incidence_coefficients.shape[1]
     cols = var_feat.shape[0] // size
     rows = con_feat.shape[0]
-    pairs = -(-(slots + cols) // 8) * 4
-    lanes = -(-max(2 * pairs, slots) // 128) * 128
+    rblocks = 2 * nc * (rows // size)
+    fpairs = -(-(slots + rblocks) // (2 * FORWARD)) * FORWARD
+    pairs = -(-(slots + cols) // (2 * BACK)) * BACK
+    lanes = -(-max(2 * pairs, 2 * fpairs, slots) // 128) * 128
     chunks = slots // CHUNK
-    dims = (nb, nc, slots, size, cols, pairs, lanes, chunks)
+    dims = (nb, nc, slots, size, cols, fpairs, pairs, lanes, chunks)
     smem = pl.BlockSpec(memory_space=pltpu.SMEM)
     vmem = pl.BlockSpec(memory_space=pltpu.VMEM)
     hbm = pl.BlockSpec(memory_space=pl.ANY)
@@ -337,8 +338,7 @@
         scratch_shapes=[
             pltpu.VMEM((slots, size, size), jnp.int32),
             pltpu.VMEM((slots + 1, size, size), BF16),
-            pltpu.VMEM((slots + 1, size, width), F32),
-            pltpu.VMEM((max(slots, pairs), size, width), F32),
+            pltpu.VMEM((max(fpairs, pairs), size, width), F32),
             pltpu.VMEM((pairs, size, 2 * size), BF16),
             pltpu.VMEM((cols, size, width), BF16),
             pltpu.VMEM((cols, size, width), BF16),
@@ -351,7 +351,7 @@
             pltpu.SemaphoreType.DMA((chunks,)),
             pltpu.SemaphoreType.DMA,
             pltpu.SemaphoreType.DMA,
-            pltpu.SemaphoreType.DMA((cols // 2,)),
+            pltpu.SemaphoreType.DMA((cols // STEP,)),
             pltpu.SemaphoreType.DMA((2 * nc,)),
             pltpu.SemaphoreType.DMA((2 * nc,)),
             pltpu.SemaphoreType.DMA((2 * nc,)),

time: 48.6 us -> 35.4 us (0.73)
  Pallas kernels: 43.2 us -> 30 us
    pallas_call x1, Pallas kernels: 43.2 us -> 30 us  [on_device(): pl.pallas_call(functools.partial(kernel, dims), out_shape=(jax.ShapeDtype...]
where the time goes in v2:
time: 35.4 us; the launch traced here: 35.2 us
  Pallas kernels  30 us (85%)
  local copies, waits for them, and re-layouts  3.83 us (11%)
  between operations  1.29 us (4%)
    pallas_call x1, Pallas kernels, on_device(): pl.pallas_call(functools.partial(kernel, dims), out_shape=(jax.ShapeDtype...  30 us
    unnamed x2, local copies, waits for them, and re-layouts  3.83 us

profile of v2, /device:TPU:0, one launch (start us, length us, event | category | flops | bytes accessed | tf_op | source)
XLA Modules:
  0.0 35.2 jit_solution(599775250960645892)
XLA Ops:
  1.3 30.0 %layer.1 = (bf16[128,128]{1,0:T(8,128)(2,1)}, bf16[40,128,128]{2,1,0:T(8,128)(2,1)}) custom-call(s32[160]{0:T(256)} %cb_s.1, s32[160]{0:T(256)} %rb_s.1, s32[1,160]{1,0:T(1,128)} %bitcast.12, s32[1,160]{1,0:T(1,128)} %bitcast.13, s32[1]{0:T(128)S(6)} %copy.22.count_s, bf16[40,128,128]{2,1,0:T(8,128)(2,1)} %bitcast.11, bf16[128,128]{1,0:T(8,128)(2,1)} %cf.1, ...), custom_call_target="tpu_custom_call" | custom-call | tf_op jit(solution)/shard_map/layer/pallas_call | solution.py:330
  31.3 1.4 %copy.23 = bf16[128,128]{1,0:T(8,128)(2,1)} copy(bf16[128,128]{1,0:T(8,128)(2,1)} %get-tuple-element.8) | data formatting | bytes 65536
  32.7 2.5 %copy.24 = bf16[5120,128]{1,0:T(8,128)(2,1)} copy(bf16[5120,128]{1,0:T(8,128)(2,1)} %bitcast.10) | data formatting | bytes 2621440

commit v3 on v2

--- a/solution.py
+++ b/solution.py
@@ -14,9 +14,10 @@
 MESH = pl.DeviceIdType.MESH
 CHUNK = 16
 UNROLL = 8
-FORWARD = 12
+FORWARD = 11
 BACK = 20
 STEP = 8
+SUB = 8
 
 
 def layer_norm(values, gain, offset):
@@ -33,7 +34,7 @@
     return layer_norm(feats.astype(F32) + output, gain, offset).astype(BF16)
 
 
-def order_rows(key_row, key_col, other_col, live_row, live_col, lanes, group):
+def order_rows(key_row, key_col, other_col, live_row, live_col, lanes, low, start):
     slots = key_col.shape[0]
     iota = lambda shape, axis: lax.broadcasted_iota(jnp.int32, shape, axis)
     lane = iota((slots, lanes), 1)
@@ -41,18 +42,20 @@
     within = jnp.sum(jnp.where(before, live_row, 0), axis=1, keepdims=True)
     counts = jnp.sum(jnp.where(lane == key_col, live_col, 0), axis=0, keepdims=True)
     counts_col = jnp.sum(jnp.where(iota((lanes, slots), 0) == key_row, live_row, 0), axis=1, keepdims=True)
-    steps, steps_col = counts, counts_col
-    if group == 2:
-        steps, steps_col = (counts + 1) >> 1, (counts_col + 1) >> 1
-    base_col = jnp.sum(jnp.where(lane < key_col, steps, 0), axis=1, keepdims=True)
-    place = jnp.where(live_col > 0, base_col * group + within, -1)
+    steps, steps_col = (counts + 1) >> 1, (counts_col + 1) >> 1
+    floor = jnp.where(key_col >= low, low, 0)
+    chosen = (lane < key_col) & (lane >= floor)
+    base_col = jnp.sum(jnp.where(chosen, steps, 0), axis=1, keepdims=True) + jnp.where(key_col >= low, start, 0)
+    place = jnp.where(live_col > 0, base_col * 2 + within, -1)
     hit = place == lane
     index = jnp.sum(jnp.where(hit, iota((slots, lanes), 0) - slots, 0), axis=0, keepdims=True) + slots
     other = jnp.sum(jnp.where(hit, other_col, 0), axis=0, keepdims=True)
-    opens = (place == lane * group) & (within == 0)
+    opens = (place == lane * 2) & (within == 0)
     carry = 1 - jnp.sum(jnp.where(opens, 1, 0), axis=0, keepdims=True)
-    upto = iota((lanes, lanes), 0) <= iota((lanes, lanes), 1)
+    above, below = iota((lanes, lanes), 0), iota((lanes, lanes), 1)
+    upto = (above <= below) & ((above >= low) == (below >= low))
     ends = jnp.sum(jnp.where(upto, steps_col, 0), axis=0, keepdims=True)
+    ends += jnp.where(iota((1, lanes), 1) >= low, start, 0)
     last = jnp.maximum(ends - 1, 0)
     filled = jnp.where(counts > 0, 1, 0)
     return [index, other, carry, last, filled]
@@ -105,10 +108,14 @@
     col_c = jnp.sum(jnp.where(diagonal, row_c, 0), axis=1, keepdims=True)
     col_r = jnp.sum(jnp.where(diagonal, row_r, 0), axis=1, keepdims=True)
     count = count_s[0]
+    early = chunks // 2 * CHUNK
     live_row = jnp.where(lax.broadcasted_iota(jnp.int32, (1, slots), 1) < count, 1, 0)
     live_col = jnp.where(lax.broadcasted_iota(jnp.int32, (slots, 1), 0) < count, 1, 0)
-    rows = order_rows(row_r, col_r, col_c, live_row, live_col, lanes, 2)
-    rows += order_rows(row_c, col_c, col_r, live_row, live_col, lanes, 2)
+    keys = 2 * nc * (part.shape[1] // size)
+    late_row = jnp.where(lax.broadcasted_iota(jnp.int32, (1, slots), 1) >= early, keys, 0)
+    late_col = jnp.where(lax.broadcasted_iota(jnp.int32, (slots, 1), 0) >= early, keys, 0)
+    rows = order_rows(row_r + late_row, col_r + late_col, col_c, live_row, live_col, lanes, keys, fpairs // 2)
+    rows += order_rows(row_c, col_c, col_r, live_row, live_col, lanes, lanes, 0)
     rows += [jnp.zeros((1, lanes), jnp.int32)] * (16 - len(rows))
     order_v[...] = jnp.concatenate(rows, axis=0)
     order_copy = pltpu.make_async_copy(order_v, order_s, order_sem)
@@ -136,7 +143,7 @@
         lax.fori_loop(0, CHUNK // UNROLL, some, 0)
         return 0
 
-    lax.fori_loop(0, chunks, convert, 0)
+    lax.fori_loop(0, chunks // 2, convert, 0)
     feat_copy.wait()
     order_copy.wait()
 
@@ -150,14 +157,19 @@
             scan[at] = carry
         return carry
 
-    lax.fori_loop(0, fpairs // FORWARD, forward, jnp.zeros(scan.shape[1:], F32))
+    turns = fpairs // FORWARD
+    carry = lax.fori_loop(0, turns // 2, forward, jnp.zeros(scan.shape[1:], F32))
+    lax.fori_loop(chunks // 2, chunks, convert, 0)
+    lax.fori_loop(turns // 2, turns, forward, carry)
 
     blocks = part.shape[1] // size
 
     def fill(q):
         for e in range(blocks):
             r = q * blocks + e
-            part[q, e * size : (e + 1) * size] = (scan[order_s[3, r]] * order_s[4, r].astype(F32)).astype(BF16)
+            sums = scan[order_s[3, r]] * order_s[4, r].astype(F32)
+            sums += scan[order_s[3, keys + r]] * order_s[4, keys + r].astype(F32)
+            part[q, e * size : (e + 1) * size] = sums.astype(BF16)
 
     def part_send(d, ahead):
         to = lax.rem(cut + d, nc)
@@ -277,15 +289,14 @@
         return pltpu.make_async_copy(result.at[piece], var_out.at[piece], out_sem.at[i])
 
     def update(i, _):
-        for u in range(0, STEP, 2):
+        for u in range(0, STEP, SUB):
             c = i * STEP + u
-            feats = jnp.concatenate([feat[c], feat[c + 1]], axis=0)
-            aggs = [scan[order_s[8, c + e]] * (order_s[9, c + e].astype(F32) * scale) for e in range(2)]
+            feats = feat[pl.ds(c, SUB)].reshape(SUB * size, -1)
+            aggs = [scan[order_s[8, c + e]] * (order_s[9, c + e].astype(F32) * scale) for e in range(SUB)]
             new = node_update(
                 feats, jnp.concatenate(aggs, axis=0),
                 vw1[...], vbias[...], vw2[...], vw3[...], vgain[...], vshift[...])
-            result[c] = new[:size]
-            result[c + 1] = new[size:]
+            result[pl.ds(c, SUB)] = new.reshape(SUB, size, -1)
         out_copy(i).start()
         return 0
 
@@ -318,9 +329,10 @@
     cols = var_feat.shape[0] // size
     rows = con_feat.shape[0]
     rblocks = 2 * nc * (rows // size)
-    fpairs = -(-(slots + rblocks) // (2 * FORWARD)) * FORWARD
+    early = slots // CHUNK // 2 * CHUNK
+    fpairs = -(-(slots - early + rblocks) // (2 * FORWARD)) * FORWARD * 2
     pairs = -(-(slots + cols) // (2 * BACK)) * BACK
-    lanes = -(-max(2 * pairs, 2 * fpairs, slots) // 128) * 128
+    lanes = -(-max(2 * pairs, 2 * fpairs, 2 * rblocks) // 128) * 128
     chunks = slots // CHUNK
     dims = (nb, nc, slots, size, cols, fpairs, pairs, lanes, chunks)
     smem = pl.BlockSpec(memory_space=pltpu.SMEM)

time: 35.4 us -> 34.4 us (0.972)
  Pallas kernels: 30 us -> 29 us
    pallas_call x1, Pallas kernels: 30 us -> 29 us  [on_device(): pl.pallas_call(functools.partial(kernel, dims), out_shape=(jax.ShapeDtype...]
where the time goes in v3:
time: 34.4 us; the launch traced here: 34.1 us
  Pallas kernels  29 us (84%)
  local copies, waits for them, and re-layouts  3.83 us (11%)
  between operations  1.29 us (4%)
    pallas_call x1, Pallas kernels, on_device(): pl.pallas_call(functools.partial(kernel, dims), out_shape=(jax.ShapeDtype...  29 us
    unnamed x2, local copies, waits for them, and re-layouts  3.83 us

profile of v3, /device:TPU:0, one launch (start us, length us, event | category | flops | bytes accessed | tf_op | source)
XLA Modules:
  0.0 34.1 jit_solution(15756887145943020946)
XLA Ops:
  1.3 29.0 %layer.1 = (bf16[128,128]{1,0:T(8,128)(2,1)}, bf16[40,128,128]{2,1,0:T(8,128)(2,1)}) custom-call(s32[160]{0:T(256)} %cb_s.1, s32[160]{0:T(256)} %rb_s.1, s32[1,160]{1,0:T(1,128)} %bitcast.12, s32[1,160]{1,0:T(1,128)} %bitcast.13, s32[1]{0:T(128)S(6)} %copy.22.count_s, bf16[40,128,128]{2,1,0:T(8,128)(2,1)} %bitcast.11, bf16[128,128]{1,0:T(8,128)(2,1)} %cf.1, ...), custom_call_target="tpu_custom_call" | custom-call | tf_op jit(solution)/shard_map/layer/pallas_call | solution.py:342
  30.3 1.4 %copy.23 = bf16[128,128]{1,0:T(8,128)(2,1)} copy(bf16[128,128]{1,0:T(8,128)(2,1)} %get-tuple-element.8) | data formatting | bytes 65536
  31.7 2.5 %copy.24 = bf16[5120,128]{1,0:T(8,128)(2,1)} copy(bf16[5120,128]{1,0:T(8,128)(2,1)} %bitcast.10) | data formatting | bytes 2621440

commit v4 on v3

--- a/solution.py
+++ b/solution.py
@@ -14,10 +14,10 @@
 MESH = pl.DeviceIdType.MESH
 CHUNK = 16
 UNROLL = 8
-FORWARD = 11
-BACK = 20
-STEP = 8
-SUB = 8
+FORWARD = 22
+BACK = 25
+STEP = 20
+SUB = 20
 
 
 def layer_norm(values, gain, offset):

time: 34.4 us -> 32.3 us (0.939)
  Pallas kernels: 29 us -> 27 us
    pallas_call x1, Pallas kernels: 29 us -> 27 us  [on_device(): pl.pallas_call(functools.partial(kernel, dims), out_shape=(jax.ShapeDtype...]
where the time goes in v4:
time: 32.3 us; the launch traced here: 32.1 us
  Pallas kernels  27 us (84%)
  local copies, waits for them, and re-layouts  3.83 us (12%)
  between operations  1.29 us (4%)
    pallas_call x1, Pallas kernels, on_device(): pl.pallas_call(functools.partial(kernel, dims), out_shape=(jax.ShapeDtype...  27 us
    unnamed x2, local copies, waits for them, and re-layouts  3.83 us

profile of v4, /device:TPU:0, one launch (start us, length us, event | category | flops | bytes accessed | tf_op | source)
XLA Modules:
  0.0 32.1 jit_solution(671407726563045028)
XLA Ops:
  1.3 27.0 %layer.1 = (bf16[128,128]{1,0:T(8,128)(2,1)}, bf16[40,128,128]{2,1,0:T(8,128)(2,1)}) custom-call(s32[160]{0:T(256)} %cb_s.1, s32[160]{0:T(256)} %rb_s.1, s32[1,160]{1,0:T(1,128)} %bitcast.12, s32[1,160]{1,0:T(1,128)} %bitcast.13, s32[1]{0:T(128)S(6)} %copy.22.count_s, bf16[40,128,128]{2,1,0:T(8,128)(2,1)} %bitcast.11, bf16[128,128]{1,0:T(8,128)(2,1)} %cf.1, ...), custom_call_target="tpu_custom_call" | custom-call | tf_op jit(solution)/shard_map/layer/pallas_call | solution.py:342
  28.3 1.4 %copy.23 = bf16[128,128]{1,0:T(8,128)(2,1)} copy(bf16[128,128]{1,0:T(8,128)(2,1)} %get-tuple-element.8) | data formatting | bytes 65536
  29.6 2.5 %copy.24 = bf16[5120,128]{1,0:T(8,128)(2,1)} copy(bf16[5120,128]{1,0:T(8,128)(2,1)} %bitcast.10) | data formatting | bytes 2621440

commit v5 on v4

--- a/solution.py
+++ b/solution.py
@@ -16,8 +16,8 @@
 UNROLL = 8
 FORWARD = 22
 BACK = 25
-STEP = 20
-SUB = 20
+STEP = 10
+GATHER = 8
 
 
 def layer_norm(values, gain, offset):
@@ -66,8 +66,7 @@
     cb_s, rb_s, cb_v, rb_v, count_s,
     vf_hbm, cf, coef_hbm,
     cw1, cbias, cw2, cw3, cgain, cshift,
-    vw1, vbias, vw2, vw3, vgain, vshift,
-    con_out, var_out,
+    con_out, agg_out,
     raw, half, scan, paired, feat, result, part, arrive, window, conbuf,
     order_v, order_s,
     raw_sem, feat_sem, order_sem, out_sem, psend, precv, wsend, wrecv,
@@ -285,22 +284,17 @@
 
     scale = 1.0 / math.sqrt(4 * size)
     def out_copy(i):
-        piece = pl.ds(i * STEP, STEP)
-        return pltpu.make_async_copy(result.at[piece], var_out.at[piece], out_sem.at[i])
-
-    def update(i, _):
-        for u in range(0, STEP, SUB):
-            c = i * STEP + u
-            feats = feat[pl.ds(c, SUB)].reshape(SUB * size, -1)
-            aggs = [scan[order_s[8, c + e]] * (order_s[9, c + e].astype(F32) * scale) for e in range(SUB)]
-            new = node_update(
-                feats, jnp.concatenate(aggs, axis=0),
-                vw1[...], vbias[...], vw2[...], vw3[...], vgain[...], vshift[...])
-            result[pl.ds(c, SUB)] = new.reshape(SUB, size, -1)
+        piece = pl.ds(i * GATHER, GATHER)
+        return pltpu.make_async_copy(result.at[piece], agg_out.at[piece], out_sem.at[i])
+
+    def gather(i, _):
+        for u in range(GATHER):
+            c = i * GATHER + u
+            result[c] = (scan[order_s[8, c]] * (order_s[9, c].astype(F32) * scale)).astype(BF16)
         out_copy(i).start()
         return 0
 
-    lax.fori_loop(0, cols // STEP, update, 0)
+    lax.fori_loop(0, cols // GATHER, gather, 0)
 
     @pl.when(has_prev)
     def _():
@@ -314,7 +308,16 @@
         out_copy(i).wait()
         return 0
 
-    lax.fori_loop(0, cols // STEP, finish, 0)
+    lax.fori_loop(0, cols // GATHER, finish, 0)
+
+
+def column_kernel(feat, agg, con, vw1, vbias, vw2, vw3, vgain, vshift, con_out, var_out):
+    @pl.when(pl.program_id(0) == 0)
+    def _():
+        con_out[...] = con[...]
+
+    var_out[...] = node_update(
+        feat[...], agg[...], vw1[...], vbias[...], vw2[...], vw3[...], vgain[...], vshift[...])
 
 
 def on_device(
@@ -339,13 +342,13 @@
     vmem = pl.BlockSpec(memory_space=pltpu.VMEM)
     hbm = pl.BlockSpec(memory_space=pl.ANY)
     row = lambda v: v.reshape(1, -1)
-    con_new, var_new = pl.pallas_call(
+    con_new, agg = pl.pallas_call(
         functools.partial(kernel, dims),
         out_shape=(
             jax.ShapeDtypeStruct(con_feat.shape, BF16),
             jax.ShapeDtypeStruct((cols, size, width), BF16),
         ),
-        in_specs=[smem, smem, vmem, vmem, smem, hbm, vmem, hbm] + [vmem] * 12,
+        in_specs=[smem, smem, vmem, vmem, smem, hbm, vmem, hbm] + [vmem] * 6,
         out_specs=(vmem, hbm),
         scratch_shapes=[
             pltpu.VMEM((slots, size, size), jnp.int32),
@@ -363,7 +366,7 @@
             pltpu.SemaphoreType.DMA((chunks,)),
             pltpu.SemaphoreType.DMA,
             pltpu.SemaphoreType.DMA,
-            pltpu.SemaphoreType.DMA((cols // STEP,)),
+            pltpu.SemaphoreType.DMA((cols // GATHER,)),
             pltpu.SemaphoreType.DMA((2 * nc,)),
             pltpu.SemaphoreType.DMA((2 * nc,)),
             pltpu.SemaphoreType.DMA((2 * nc,)),
@@ -376,9 +379,22 @@
         slot_column_block, slot_constraint_block, row(slot_column_block), row(slot_constraint_block), block_count,
         var_feat.reshape(cols, size, width), con_feat, incidence_coefficients,
         con_first, row(con_bias), con_second, con_third, row(con_gain), row(con_shift),
-        var_first, row(var_bias), var_second, var_third, row(var_gain), row(var_shift),
     )
-    return con_new, var_new.reshape(var_feat.shape)
+    weights = (var_first, row(var_bias), var_second, var_third, row(var_gain), row(var_shift))
+    moving = pl.BlockSpec((STEP * size, width), lambda i: (i, 0))
+    still = lambda v: pl.BlockSpec(v.shape, lambda i: (0, 0))
+    return pl.pallas_call(
+        column_kernel,
+        grid=(cols // STEP,),
+        out_shape=(
+            jax.ShapeDtypeStruct(con_feat.shape, BF16),
+            jax.ShapeDtypeStruct(var_feat.shape, BF16),
+        ),
+        in_specs=[moving, moving, still(con_new)] + [still(w) for w in weights],
+        out_specs=(still(con_new), moving),
+        compiler_params=pltpu.CompilerParams(vmem_limit_bytes=63 * 1024 * 1024),
+        name="columns",
+    )(var_feat, agg.reshape(var_feat.shape), con_new, *weights)
 
 
 def solution(mesh):

time: 32.3 us -> 31.5 us (0.975)
  local copies, waits for them, and re-layouts: 3.83 us -> 0 us
  Pallas kernels: 27 us -> 30 us
    pallas_call x0 -> x1, Pallas kernels: none -> 6.11 us  [on_device(): pl.pallas_call(column_kernel, grid=(cols // STEP,), out_shape=(jax.ShapeD...]
    unnamed x2 -> x0, local copies, waits for them, and re-layouts: 3.83 us -> none
    pallas_call x1, Pallas kernels: 27 us -> 23.9 us  [on_device(): pl.pallas_call(functools.partial(kernel, dims), out_shape=(jax.ShapeDtype...]
where the time goes in v5:
time: 31.5 us; the launch traced here: 31.3 us
  Pallas kernels  30 us (95%)
  between operations  1.29 us (4%)
    pallas_call x1, Pallas kernels, on_device(): pl.pallas_call(functools.partial(kernel, dims), out_shape=(jax.ShapeDtype...  23.9 us
    pallas_call x1, Pallas kernels, on_device(): pl.pallas_call(column_kernel, grid=(cols // STEP,), out_shape=(jax.ShapeD...  6.11 us

profile of v5, /device:TPU:0, one launch (start us, length us, event | category | flops | bytes accessed | tf_op | source)
XLA Modules:
  0.0 31.3 jit_solution(3653318673264582946)
XLA Ops:
  1.3 23.9 %layer.1 = (bf16[128,128]{1,0:T(8,128)(2,1)}, bf16[40,128,128]{2,1,0:T(8,128)(2,1)}) custom-call(s32[160]{0:T(256)} %cb_s.1, s32[160]{0:T(256)} %rb_s.1, s32[1,160]{1,0:T(1,128)} %bitcast.12, s32[1,160]{1,0:T(1,128)} %bitcast.13, s32[1]{0:T(128)S(6)} %copy.20.count_s, bf16[40,128,128]{2,1,0:T(8,128)(2,1)} %bitcast.10, bf16[128,128]{1,0:T(8,128)(2,1)} %cf.1, ...), custom_call_target="tpu_custom_call" | custom-call | tf_op jit(solution)/shard_map/layer/pallas_call | solution.py:345
  25.2 6.1 %columns.1 = (bf16[128,128]{1,0:T(8,128)(2,1)}, bf16[5120,128]{1,0:T(8,128)(2,1)}) custom-call(bf16[5120,128]{1,0:T(8,128)(2,1)} %feat.1, bf16[5120,128]{1,0:T(8,128)(2,1)} %bitcast.11, bf16[128,128]{1,0:T(8,128)(2,1)} %get-tuple-element.5.con, bf16[256,256]{1,0:T(8,128)(2,1)} %vw1.1, f32[1,256]{1,0:T(1,128)} %bitcast.14, bf16[256,256]{1,0:T(8,128)(2,1)} %vw2.1, ...), custom_call_target="tpu_custom_call" | custom-call | tf_op jit(solution)/shard_map/columns/pallas_call | solution.py:386
